TPU v7x, 32 devices: a whole 2x2x4 slice. The times are simulated.
32 devices in a mesh: fsdp: 8 (over z, x), tp: 4 (over y, core).
Axes of the slice: x: 2, y: 2, z: 4, core: 2. Of those that a mesh axis runs over, the one named last changes fastest.
Arguments:
- tokens: bfloat16 [8192, 1024], P(('fsdp', 'tp')), may hold values from -6 to 6
- lengths: int32 [4], replicated, may hold values from 1 to 4096, 8192 in all
- attn_gain: bfloat16 [1024], P('fsdp'), may hold values from 0.5 to 1.5
- w_query: bfloat16 [1024, 1024], P('fsdp', 'tp'), may hold values from -0.1875 to 0.1875
- w_key: bfloat16 [1024, 1024], P('fsdp', 'tp'), may hold values from -0.1875 to 0.1875
- w_value: bfloat16 [1024, 2048], P('fsdp', 'tp'), may hold values from -0.1875 to 0.1875
- w_gate_out: bfloat16 [1024, 2048], P('fsdp', 'tp'), may hold values from -0.1875 to 0.1875
- w_beta: bfloat16 [1024, 8], P('fsdp', 'tp'), may hold values from -0.1875 to 0.1875
- w_decay: bfloat16 [1024, 8], P('fsdp', 'tp'), may hold values from -0.1875 to 0.1875
- conv_query: bfloat16 [4, 8, 128], P(None, 'tp', 'fsdp'), may hold values from -2.5 to 2.5
- conv_key: bfloat16 [4, 8, 128], P(None, 'tp', 'fsdp'), may hold values from -2.5 to 2.5
- conv_value: bfloat16 [4, 8, 256], P(None, 'tp', 'fsdp'), may hold values from -2.5 to 2.5
- decay_log: float32 [8], P('tp'), may hold values from -6 to -1
- decay_bias: float32 [8], P('tp'), may hold values from -1.5 to 0.5
- out_gain: bfloat16 [256], P('fsdp'), may hold values from 0.5 to 1.5
- w_out: bfloat16 [2048, 1024], P('tp', 'fsdp'), may hold values from -0.25 to 0.25
- ffn_gain: bfloat16 [1024], P('fsdp'), may hold values from 0.5 to 1.5
- w_ffn_gate: bfloat16 [1024, 2816], P('fsdp', 'tp'), may hold values from -0.1875 to 0.1875
- w_ffn_up: bfloat16 [1024, 2816], P('fsdp', 'tp'), may hold values from -0.1875 to 0.1875
- w_ffn_down: bfloat16 [2816, 1024], P('tp', 'fsdp'), may hold values from -0.21875 to 0.21875
- cotangent: bfloat16 [8192, 1024], P(('fsdp', 'tp')), may hold values from -6 to 6
Outputs:
- output: float32 [8192, 1024], P(('fsdp', 'tp'))
- d_tokens: float32 [8192, 1024], P(('fsdp', 'tp'))
- grad_attn_gain: float32 [1024], P('fsdp')
- grad_w_query: float32 [1024, 1024], P('fsdp', 'tp')
- grad_w_key: float32 [1024, 1024], P('fsdp', 'tp')
- grad_w_value: float32 [1024, 2048], P('fsdp', 'tp')
- grad_w_gate_out: float32 [1024, 2048], P('fsdp', 'tp')
- grad_w_beta: float32 [1024, 8], P('fsdp', 'tp')
- grad_w_decay: float32 [1024, 8], P('fsdp', 'tp')
- grad_conv_query: float32 [4, 8, 128], P(None, 'tp', 'fsdp')
- grad_conv_key: float32 [4, 8, 128], P(None, 'tp', 'fsdp')
- grad_conv_value: float32 [4, 8, 256], P(None, 'tp', 'fsdp')
- grad_decay_log: float32 [8], P('tp')
- grad_decay_bias: float32 [8], P('tp')
- grad_out_gain: float32 [256], P('fsdp')
- grad_w_out: float32 [2048, 1024], P('tp', 'fsdp')
- grad_ffn_gain: float32 [1024], P('fsdp')
- grad_w_ffn_gate: float32 [1024, 2816], P('fsdp', 'tp')
- grad_w_ffn_up: float32 [1024, 2816], P('fsdp', 'tp')
- grad_w_ffn_down: float32 [2816, 1024], P('tp', 'fsdp')
Inputs may be any that keep to these rules, and one draw needn't show every extreme that they name: The 4 lengths sum to 8192; the largest is exactly 4096.
All inputs are finite; a program needn't handle non-finite values.
Results may differ from a plain program's by a relative error of at most 0.03.
Values may be sent and summed in bfloat16 or wider, within the bound.
A program may use at most 256 MiB of HBM per device.

v0:
```python
import jax
import jax.numpy as jnp
from jax import lax
from jax.sharding import PartitionSpec as P

K = 128
V = 256
CONV = 4
GROUP = 64


highest = lax.Precision.HIGHEST


def shifted(array, axis, by):
    count = lax.axis_size(axis)
    pairs = [(i, i + by) for i in range(count) if 0 <= i + by < count]
    return lax.ppermute(array, axis, pairs)


def entering(value, axis, join, neutral):
    count, mine = (lax.axis_size(axis), lax.axis_index(axis))
    pieces = jax.tree.map(lambda part: lax.all_gather(part, axis), value)
    so_far = jax.tree.map(
        lambda part, zero: jnp.full_like(part, 0) + jnp.asarray(zero, part.dtype), value, neutral
    )

    def hop(position, so_far):
        longer = join(so_far, jax.tree.map(lambda part: part[position], pieces))
        return jax.tree.map(lambda new, old: jnp.where(position < mine, new, old), longer, so_far)

    return lax.fori_loop(0, count - 1, hop, so_far)


def carried_in(array, axis, join, neutral):
    count = lax.axis_size(axis)
    place = lax.axis_index(axis)
    ahead = count - 1 - place
    gathered = jax.tree.map(
        lambda a, kind: lax.all_gather(a.astype(kind), axis),
        array,
        jax.tree.map(lambda a: jnp.bfloat16 if a.dtype == jnp.float32 else a.dtype, array),
    )
    state = jax.tree.map(lambda a, e: jnp.zeros_like(a) + jnp.asarray(e, a.dtype), array, neutral)

    def one(hop, state):
        source = count - 1 - hop
        return join(
            state,
            jax.tree.map(
                lambda a, own: lax.dynamic_index_in_dim(a, source, 0, False).astype(own.dtype),
                gathered,
                array,
            ),
        )

    return lax.fori_loop(0, ahead, one, state)


def mat_dot(left, right):
    return jnp.dot(left, right, preferred_element_type=jnp.float32)


def rms_scale(values, scale_gain):
    return (
        values * lax.rsqrt(jnp.mean(values * values, axis=-1, keepdims=True) + 1e-06) * scale_gain
    )


def unit_rows(values):
    return values * lax.rsqrt(jnp.sum(values * values, axis=-1, keepdims=True) + 1e-06)


def seq_begin(lengths, positions):
    offsets = jnp.cumsum(lengths) - lengths
    chosen = jnp.where(offsets[None, :] <= positions[:, None], offsets[None, :], 0)
    return jnp.max(chosen, axis=1)


def split_heads(flat, width):
    return flat.reshape(flat.shape[0], -1, width).transpose(1, 0, 2)


def merge_heads(stacked):
    return stacked.transpose(1, 0, 2).reshape(stacked.shape[1], -1)


def short_conv(inputs, rim_rows, kernel, begins, positions):
    row_count = inputs.shape[0]
    padded = jnp.concatenate([rim_rows, inputs], axis=0)
    result = kernel[0] * inputs
    for lag_step in range(1, CONV):
        in_range = (positions - lag_step >= begins).astype(inputs.dtype)[:, None]
        start_row = CONV - 1 - lag_step
        result = result + kernel[lag_step] * padded[start_row : start_row + row_count] * in_range
    return jax.nn.silu(result)


def head_inputs(
    query_raw,
    key_raw,
    value_raw,
    query_rim,
    key_rim,
    value_rim,
    query_kernel,
    key_kernel,
    value_kernel,
    beta_raw,
    decay_raw,
    decay_scale,
    decay_shift,
    begins,
    positions,
):
    query_vec = unit_rows(
        short_conv(query_raw, query_rim, query_kernel, begins, positions)
    ) * query_raw.shape[1] ** (-0.5)
    key_vec = unit_rows(short_conv(key_raw, key_rim, key_kernel, begins, positions))
    value_vec = short_conv(value_raw, value_rim, value_kernel, begins, positions)
    beta_gate = jax.nn.sigmoid(beta_raw)
    decay_rate = -jnp.exp(decay_scale) * jax.nn.softplus(decay_raw + decay_shift)
    return (query_vec, key_vec, value_vec, beta_gate, decay_rate)


def block_terms(query_vec, key_vec, value_vec, beta_gate, decay_rate, begins, positions):
    blocks = query_vec.shape[0] // GROUP
    query_block = query_vec.reshape(blocks, GROUP, -1)
    key_block = key_vec.reshape(blocks, GROUP, -1)
    value_block = value_vec.reshape(blocks, GROUP, -1)
    beta_block = beta_gate.reshape(blocks, GROUP)
    decay_block = decay_rate.reshape(blocks, GROUP)
    begin_block = begins.reshape(blocks, GROUP)
    place_block = positions.reshape(blocks, GROUP)
    cumul = jnp.cumsum(decay_block, axis=1)
    same_seq = (begin_block[:, :, None] <= place_block[:, None, :]) & (
        place_block[:, None, :] <= place_block[:, :, None]
    )
    same_float = same_seq.astype(query_vec.dtype)
    factor = jnp.exp(jnp.where(same_seq, cumul[:, :, None] - cumul[:, None, :], 0.0)) * same_float
    alive_mask = (begin_block < place_block[:, :1]).astype(query_vec.dtype)
    carry_scale = jnp.exp(cumul) * alive_mask
    strict = (place_block[:, None, :] < place_block[:, :, None]).astype(query_vec.dtype)
    key_gram = jnp.einsum("ntd,nsd->nts", key_block, key_block, precision=highest)
    lower_mat = (
        jnp.eye(GROUP, dtype=query_vec.dtype)[None]
        + beta_block[:, :, None] * key_gram * factor * strict
    )
    value_part = lax.linalg.triangular_solve(
        lower_mat,
        beta_block[:, :, None] * value_block,
        left_side=True,
        lower=True,
        unit_diagonal=True,
    )
    key_part = lax.linalg.triangular_solve(
        lower_mat,
        (beta_block * carry_scale)[:, :, None] * key_block,
        left_side=True,
        lower=True,
        unit_diagonal=True,
    )
    scores = jnp.einsum("ntd,nsd->nts", query_block, key_block, precision=highest) * factor
    key_last = key_block * factor[:, -1, :, None]
    return (query_block, carry_scale, scores, value_part, key_part, key_last)


def state_run(carry_scale, value_part, key_part, key_last):
    identity_mat = jnp.eye(key_part.shape[-1], dtype=key_part.dtype)

    def advance(carry, pieces):
        matrix, offset = carry
        scale_block, value_block, key_block, last_block = pieces
        transfer = scale_block[-1] * identity_mat - jnp.dot(
            last_block.T, key_block, precision=highest
        )
        new_matrix = jnp.dot(transfer, matrix, precision=highest)
        new_offset = jnp.dot(transfer, offset, precision=highest) + jnp.dot(
            last_block.T, value_block, precision=highest
        )
        return ((new_matrix, new_offset), (matrix, offset))

    start_pair = (
        identity_mat,
        jnp.zeros((identity_mat.shape[0], value_part.shape[-1]), key_part.dtype),
    )
    final_pair, stacked = lax.scan(
        advance, start_pair, (carry_scale, value_part, key_part, key_last)
    )
    return (stacked[0], stacked[1], final_pair[0], final_pair[1])


def compose(early, late):
    matrix = jnp.einsum("hij,hjk->hik", late[0], early[0], precision=highest)
    offset = jnp.einsum("hij,hjv->hiv", late[0], early[1], precision=highest) + late[1]
    return (matrix, offset)


def front_all(
    mixed_raw,
    rim_raw,
    query_kernel,
    key_kernel,
    value_kernel,
    beta_raw,
    decay_raw,
    decay_scale,
    decay_shift,
    begins,
    positions,
    head_count,
):
    query_width = head_count * K

    def front_one_head(
        query_raw,
        key_raw,
        value_raw,
        query_rim,
        key_rim,
        value_rim,
        query_taps,
        key_taps,
        value_taps,
        beta_head,
        decay_head,
        scale_head,
        shift_head,
    ):
        inputs = head_inputs(
            query_raw,
            key_raw,
            value_raw,
            query_rim,
            key_rim,
            value_rim,
            query_taps,
            key_taps,
            value_taps,
            beta_head,
            decay_head,
            scale_head,
            shift_head,
            begins,
            positions,
        )
        block_parts = block_terms(*inputs, begins, positions)
        state_parts = state_run(block_parts[1], block_parts[3], block_parts[4], block_parts[5])
        return (block_parts, state_parts)

    block_parts, state_parts = jax.vmap(front_one_head)(
        split_heads(mixed_raw[:, :query_width], K),
        split_heads(mixed_raw[:, query_width : 2 * query_width], K),
        split_heads(mixed_raw[:, 2 * query_width :], V),
        split_heads(rim_raw[:, :query_width], K),
        split_heads(rim_raw[:, query_width : 2 * query_width], K),
        split_heads(rim_raw[:, 2 * query_width :], V),
        jnp.transpose(query_kernel, (1, 0, 2)),
        jnp.transpose(key_kernel, (1, 0, 2)),
        jnp.transpose(value_kernel, (1, 0, 2)),
        beta_raw.T,
        decay_raw.T,
        decay_scale,
        decay_shift,
    )
    return (block_parts, state_parts[0], state_parts[1], state_parts[2], state_parts[3])


def back_all(block_parts, prefix_mat, prefix_off, state_in, gate_heads, out_scale):

    def back_one_head(parts, matrix, offset, state_now, gate_now):
        query_block, carry_scale, scores, value_part, key_part, key_last = parts
        start_state = jnp.einsum("nij,jv->niv", matrix, state_now, precision=highest) + offset
        update = value_part - jnp.einsum("ncj,njv->ncv", key_part, start_state, precision=highest)
        outputs = carry_scale[:, :, None] * jnp.einsum(
            "ncj,njv->ncv", query_block, start_state, precision=highest
        )
        outputs = outputs + jnp.einsum("nts,nsv->ntv", scores, update, precision=highest)
        outputs = outputs.reshape(-1, outputs.shape[-1])
        return rms_scale(outputs, out_scale) * jax.nn.silu(gate_now)

    return jax.vmap(back_one_head)(block_parts, prefix_mat, prefix_off, state_in, gate_heads)


def shards(
    tokens,
    lengths,
    attn_gain,
    w_query,
    w_key,
    w_value,
    w_gate_out,
    w_beta,
    w_decay,
    conv_query,
    conv_key,
    conv_value,
    decay_log,
    decay_bias,
    out_gain,
    w_out,
    ffn_gain,
    w_ffn_gate,
    w_ffn_up,
    w_ffn_down,
    cotangent,
):
    gathered = (
        lax.all_gather(attn_gain, "fsdp", axis=0, tiled=True),
        lax.all_gather(w_query, "fsdp", axis=0, tiled=True),
        lax.all_gather(w_key, "fsdp", axis=0, tiled=True),
        lax.all_gather(w_value, "fsdp", axis=0, tiled=True),
        lax.all_gather(w_gate_out, "fsdp", axis=0, tiled=True),
        lax.all_gather(w_beta, "fsdp", axis=0, tiled=True),
        lax.all_gather(w_decay, "fsdp", axis=0, tiled=True),
        lax.all_gather(conv_query, "fsdp", axis=2, tiled=True),
        lax.all_gather(conv_key, "fsdp", axis=2, tiled=True),
        lax.all_gather(conv_value, "fsdp", axis=2, tiled=True),
        lax.all_gather(out_gain, "fsdp", axis=0, tiled=True),
        lax.all_gather(w_out, "fsdp", axis=1, tiled=True),
        lax.all_gather(ffn_gain, "fsdp", axis=0, tiled=True),
        lax.all_gather(w_ffn_gate, "fsdp", axis=0, tiled=True),
        lax.all_gather(w_ffn_up, "fsdp", axis=0, tiled=True),
        lax.all_gather(w_ffn_down, "fsdp", axis=1, tiled=True),
    )
    (
        gain_one,
        query_w,
        key_w,
        value_w,
        gate_w,
        beta_w,
        decay_w,
        query_taps,
        key_taps,
        value_taps,
        norm_out,
        out_w,
        gain_two,
        ffn_gate_w,
        ffn_up_w,
        ffn_down_w,
    ) = gathered
    seq_rows, cot_rows = (
        lax.all_gather(tokens, "tp", axis=0, tiled=True),
        lax.all_gather(cotangent, "tp", axis=0, tiled=True),
    )
    row_count = seq_rows.shape[0]
    shard_rows = tokens.shape[0]
    head_count = query_w.shape[1] // K
    query_width = head_count * K
    positions = lax.axis_index("fsdp") * row_count + jnp.arange(row_count, dtype=jnp.int32)
    begins = seq_begin(lengths, positions)
    rows_float = seq_rows.astype(jnp.float32)
    normed_one, pull_one = jax.vjp(rms_scale, rows_float, gain_one.astype(jnp.float32))
    normed_one = normed_one.astype(jnp.bfloat16)
    mixed_raw = jnp.concatenate(
        [
            mat_dot(normed_one, query_w).astype(jnp.bfloat16),
            mat_dot(normed_one, key_w).astype(jnp.bfloat16),
            mat_dot(normed_one, value_w).astype(jnp.bfloat16),
        ],
        axis=1,
    )
    gate_raw = mat_dot(normed_one, gate_w)
    beta_raw = mat_dot(normed_one, beta_w)
    decay_raw = mat_dot(normed_one, decay_w)
    rim_recv = shifted(mixed_raw[row_count - (CONV - 1) :], "fsdp", 1)

    def front_local(
        mixed_in, rim_in, query_in, key_in, value_in, beta_in, decay_in, scale_in, shift_in
    ):
        return front_all(
            mixed_in,
            rim_in,
            query_in,
            key_in,
            value_in,
            beta_in,
            decay_in,
            scale_in,
            shift_in,
            begins,
            positions,
            head_count,
        )

    front_out, pull_front = jax.vjp(
        front_local,
        mixed_raw.astype(jnp.float32),
        rim_recv.astype(jnp.float32),
        query_taps.astype(jnp.float32),
        key_taps.astype(jnp.float32),
        value_taps.astype(jnp.float32),
        beta_raw,
        decay_raw,
        decay_log,
        decay_bias,
    )
    block_parts, prefix_mat, prefix_off, final_mat, final_off = front_out
    identity_pair = (
        jnp.broadcast_to(jnp.eye(K, dtype=jnp.float32), final_mat.shape),
        jnp.zeros_like(final_off),
    )
    _, state_in = entering((final_mat, final_off), "fsdp", compose, identity_pair)
    mixer_out, pull_back = jax.vjp(
        back_all,
        block_parts,
        prefix_mat,
        prefix_off,
        state_in,
        split_heads(gate_raw, V),
        norm_out.astype(jnp.float32),
    )
    normed_mixer = merge_heads(mixer_out).astype(jnp.bfloat16)
    mixer_part = mat_dot(normed_mixer, out_w)
    tp_index = lax.axis_index("tp")
    mixer_own = lax.psum_scatter(mixer_part, "tp", scatter_dimension=0, tiled=True)
    hidden_part = tokens.astype(jnp.float32) + mixer_own
    hidden_rows = lax.all_gather(hidden_part, "tp", axis=0, tiled=True)
    hidden_own = lax.dynamic_slice_in_dim(hidden_rows, tp_index * shard_rows, shard_rows, 0)
    normed_two, pull_two = jax.vjp(rms_scale, hidden_rows, gain_two.astype(jnp.float32))
    normed_two = normed_two.astype(jnp.bfloat16)
    gate_pre = mat_dot(normed_two, ffn_gate_w)
    up_pre = mat_dot(normed_two, ffn_up_w)
    gate_sigmoid = jax.nn.sigmoid(gate_pre)
    activated = (gate_pre * gate_sigmoid * up_pre).astype(jnp.bfloat16)
    ffn_part = mat_dot(activated, ffn_down_w)
    ffn_own = lax.psum_scatter(
        ffn_part.astype(jnp.bfloat16), "tp", scatter_dimension=0, tiled=True
    ).astype(jnp.float32)
    output = hidden_own + ffn_own
    d_active = mat_dot(cot_rows, ffn_down_w.T)
    grad_down = mat_dot(activated.T, cot_rows)
    d_gate = (d_active * up_pre * gate_sigmoid * (1.0 + gate_pre * (1.0 - gate_sigmoid))).astype(
        jnp.bfloat16
    )
    d_upper = (d_active * gate_pre * gate_sigmoid).astype(jnp.bfloat16)
    grad_gate = mat_dot(normed_two.T, d_gate)
    grad_upper = mat_dot(normed_two.T, d_upper)
    d_normed_two = mat_dot(d_gate, ffn_gate_w.T) + mat_dot(d_upper, ffn_up_w.T)
    d_hidden_part, gain_two_part = pull_two(d_normed_two)
    d_hidden_own = lax.psum_scatter(d_hidden_part, "tp", scatter_dimension=0, tiled=True)
    d_hidden = cotangent.astype(jnp.float32) + d_hidden_own
    d_hidden_rows = lax.all_gather(d_hidden.astype(jnp.bfloat16), "tp", axis=0, tiled=True)
    d_mixer = mat_dot(d_hidden_rows, out_w.T)
    grad_out = mat_dot(normed_mixer.T, d_hidden_rows)
    d_parts, d_prefix_mat, d_prefix_off, d_state_in, d_gate_heads, norm_out_part = pull_back(
        split_heads(d_mixer, V)
    )
    _, d_state_out = carried_in(
        (jnp.swapaxes(final_mat, 1, 2), d_state_in), "fsdp", compose, identity_pair
    )
    d_final_mat = jnp.einsum("hiv,hjv->hij", d_state_out, state_in, precision=highest)
    front_grads = pull_front((d_parts, d_prefix_mat, d_prefix_off, d_final_mat, d_state_out))
    (
        d_mixed,
        d_rim,
        d_query_taps,
        d_key_taps,
        d_value_taps,
        d_beta_raw,
        d_decay_raw,
        d_decay_log,
        d_decay_bias,
    ) = front_grads
    rim_grad = shifted(d_rim, "fsdp", -1)
    d_mixed = d_mixed + jnp.concatenate(
        [jnp.zeros((row_count - (CONV - 1), d_mixed.shape[1]), jnp.float32), rim_grad], axis=0
    )
    d_mixed_half = d_mixed.astype(jnp.bfloat16)
    d_query_half = d_mixed_half[:, :query_width]
    d_key_half = d_mixed_half[:, query_width : 2 * query_width]
    d_value_half = d_mixed_half[:, 2 * query_width :]
    d_gate_half = merge_heads(d_gate_heads).astype(jnp.bfloat16)
    d_beta_half = d_beta_raw.astype(jnp.bfloat16)
    d_decay_half = d_decay_raw.astype(jnp.bfloat16)
    grad_query = mat_dot(normed_one.T, d_query_half)
    grad_key = mat_dot(normed_one.T, d_key_half)
    grad_value = mat_dot(normed_one.T, d_value_half)
    grad_gate_out = mat_dot(normed_one.T, d_gate_half)
    grad_beta = mat_dot(normed_one.T, d_beta_half)
    grad_decay = mat_dot(normed_one.T, d_decay_half)
    d_normed_one = (
        mat_dot(d_query_half, query_w.T)
        + mat_dot(d_key_half, key_w.T)
        + mat_dot(d_value_half, value_w.T)
        + mat_dot(d_gate_half, gate_w.T)
        + mat_dot(d_beta_half, beta_w.T)
        + mat_dot(d_decay_half, decay_w.T)
    )
    d_rows_part, gain_one_part = pull_one(d_normed_one)
    gains_part = jnp.concatenate([gain_one_part, gain_two_part, norm_out_part])
    spread_gains = jnp.broadcast_to(gains_part[None, :], (lax.axis_size("tp"), gains_part.shape[0]))
    d_input_own, gains_summed = (
        lax.psum_scatter(
            d_rows_part.astype(jnp.bfloat16), "tp", scatter_dimension=0, tiled=True
        ).astype(jnp.float32),
        lax.psum_scatter(
            spread_gains.astype(jnp.bfloat16), "tp", scatter_dimension=0, tiled=True
        ).astype(jnp.float32),
    )
    d_tokens = d_hidden + d_input_own
    width = gain_one_part.shape[0]
    decay_pair = jnp.concatenate([d_decay_log, d_decay_bias])
    spread_decay = jnp.broadcast_to(
        decay_pair[None, :], (lax.axis_size("fsdp"), decay_pair.shape[0])
    )
    summed = (
        lax.psum_scatter(
            gains_summed[0, :width].astype(jnp.bfloat16), "fsdp", scatter_dimension=0, tiled=True
        ).astype(jnp.float32),
        lax.psum_scatter(
            gains_summed[0, width : 2 * width].astype(jnp.bfloat16),
            "fsdp",
            scatter_dimension=0,
            tiled=True,
        ).astype(jnp.float32),
        lax.psum_scatter(
            gains_summed[0, 2 * width :].astype(jnp.bfloat16),
            "fsdp",
            scatter_dimension=0,
            tiled=True,
        ).astype(jnp.float32),
        lax.psum_scatter(
            grad_query.astype(jnp.bfloat16), "fsdp", scatter_dimension=0, tiled=True
        ).astype(jnp.float32),
        lax.psum_scatter(
            grad_key.astype(jnp.bfloat16), "fsdp", scatter_dimension=0, tiled=True
        ).astype(jnp.float32),
        lax.psum_scatter(
            grad_value.astype(jnp.bfloat16), "fsdp", scatter_dimension=0, tiled=True
        ).astype(jnp.float32),
        lax.psum_scatter(
            grad_gate_out.astype(jnp.bfloat16), "fsdp", scatter_dimension=0, tiled=True
        ).astype(jnp.float32),
        lax.psum_scatter(
            grad_beta.astype(jnp.bfloat16), "fsdp", scatter_dimension=0, tiled=True
        ).astype(jnp.float32),
        lax.psum_scatter(
            grad_decay.astype(jnp.bfloat16), "fsdp", scatter_dimension=0, tiled=True
        ).astype(jnp.float32),
        lax.psum_scatter(
            d_query_taps.astype(jnp.bfloat16), "fsdp", scatter_dimension=2, tiled=True
        ).astype(jnp.float32),
        lax.psum_scatter(
            d_key_taps.astype(jnp.bfloat16), "fsdp", scatter_dimension=2, tiled=True
        ).astype(jnp.float32),
        lax.psum_scatter(
            d_value_taps.astype(jnp.bfloat16), "fsdp", scatter_dimension=2, tiled=True
        ).astype(jnp.float32),
        lax.psum_scatter(
            grad_out.astype(jnp.bfloat16), "fsdp", scatter_dimension=1, tiled=True
        ).astype(jnp.float32),
        lax.psum_scatter(
            grad_gate.astype(jnp.bfloat16), "fsdp", scatter_dimension=0, tiled=True
        ).astype(jnp.float32),
        lax.psum_scatter(
            grad_upper.astype(jnp.bfloat16), "fsdp", scatter_dimension=0, tiled=True
        ).astype(jnp.float32),
        lax.psum_scatter(
            grad_down.astype(jnp.bfloat16), "fsdp", scatter_dimension=1, tiled=True
        ).astype(jnp.float32),
        lax.psum_scatter(
            spread_decay.astype(jnp.bfloat16), "fsdp", scatter_dimension=0, tiled=True
        ).astype(jnp.float32),
    )
    (
        grad_attn_gain,
        grad_ffn_gain,
        grad_out_gain,
        grad_w_query,
        grad_w_key,
        grad_w_value,
        grad_w_gate_out,
        grad_w_beta,
        grad_w_decay,
        grad_conv_query,
        grad_conv_key,
        grad_conv_value,
        grad_w_out,
        grad_w_ffn_gate,
        grad_w_ffn_up,
        grad_w_ffn_down,
        decay_summed,
    ) = summed
    grad_decay_log = decay_summed[0, :head_count]
    grad_decay_bias = decay_summed[0, head_count:]
    return (
        output,
        d_tokens,
        grad_attn_gain,
        grad_w_query,
        grad_w_key,
        grad_w_value,
        grad_w_gate_out,
        grad_w_beta,
        grad_w_decay,
        grad_conv_query,
        grad_conv_key,
        grad_conv_value,
        grad_decay_log,
        grad_decay_bias,
        grad_out_gain,
        grad_w_out,
        grad_ffn_gain,
        grad_w_ffn_gate,
        grad_w_ffn_up,
        grad_w_ffn_down,
    )


def solution(mesh):
    placed = (
        P(("fsdp", "tp"), None),
        P(),
        P("fsdp"),
        P("fsdp", "tp"),
        P("fsdp", "tp"),
        P("fsdp", "tp"),
        P("fsdp", "tp"),
        P("fsdp", "tp"),
        P("fsdp", "tp"),
        P(None, "tp", "fsdp"),
        P(None, "tp", "fsdp"),
        P(None, "tp", "fsdp"),
        P("tp"),
        P("tp"),
        P("fsdp"),
        P("tp", "fsdp"),
        P("fsdp"),
        P("fsdp", "tp"),
        P("fsdp", "tp"),
        P("tp", "fsdp"),
        P(("fsdp", "tp"), None),
    )
    return jax.shard_map(
        shards,
        mesh=mesh,
        in_specs=placed,
        out_specs=(
            P(("fsdp", "tp"), None),
            P(("fsdp", "tp"), None),
            P("fsdp"),
            P("fsdp", "tp"),
            P("fsdp", "tp"),
            P("fsdp", "tp"),
            P("fsdp", "tp"),
            P("fsdp", "tp"),
            P("fsdp", "tp"),
            P(None, "tp", "fsdp"),
            P(None, "tp", "fsdp"),
            P(None, "tp", "fsdp"),
            P("tp"),
            P("tp"),
            P("fsdp"),
            P("tp", "fsdp"),
            P("fsdp"),
            P("fsdp", "tp"),
            P("fsdp", "tp"),
            P("tp", "fsdp"),
        ),
        check_vma=False,
    )
```

profile of v0, /device:TPU:0, one launch (start us, length us, event | category | flops | bytes accessed | tf_op | source)
XLA Modules:
  0.0 2246.4 jit_solution(5175214150651427356)
XLA Ops:
  35.0 32.3 %all_gather.89 = bf16[1024,256]{1,0:T(8,128)(2,1)S(1)} all-gather(bf16[128,256]{1,0:T(8,128)(2,1)} %param.35), channel_id=1, replica_groups=mesh['fsdp'=8,'tp'=4] {'fsdp'}, dimensions={0}, use_global_device_ids=true | all-gather | bytes 589824 | tf_op jit(solution)/shard_map/all_gather | solution.py:311
  67.3 32.0 %all_gather.88 = bf16[1024,256]{1,0:T(8,128)(2,1)S(1)} all-gather(bf16[128,256]{1,0:T(8,128)(2,1)} %param.34), channel_id=1, replica_groups=mesh['fsdp'=8,'tp'=4] {'fsdp'}, dimensions={0}, use_global_device_ids=true | all-gather | bytes 589824 | tf_op jit(solution)/shard_map/all_gather | solution.py:310
  100.1 30.5 %all_gather.93 = bf16[4,2,256]{0,1,2:T(2,128)(2,1)S(1)} all-gather(bf16[4,2,32]{0,1,2:T(2,128)(2,1)S(1)} %copy.417), channel_id=1, replica_groups=mesh['fsdp'=8,'tp'=4] {'fsdp'}, dimensions={2}, use_global_device_ids=true | all-gather | bytes 4608 | tf_op jit(solution)/shard_map/all_gather | solution.py:318
  134.5 30.5 %all_gather.91 = bf16[4,2,128]{0,1,2:T(2,128)(2,1)S(1)} all-gather(bf16[4,2,16]{0,1,2:T(2,128)(2,1)S(1)} %copy.408), channel_id=1, replica_groups=mesh['fsdp'=8,'tp'=4] {'fsdp'}, dimensions={2}, use_global_device_ids=true | all-gather | bytes 2304 | tf_op jit(solution)/shard_map/all_gather | solution.py:317
  242.9 158.7 %custom-call.12 = f32[2,16,1,64,64]{3,4,2,1,0:T(8,128)} custom-call(f32[2,16,1,64,64]{4,3,2,1,0:T(8,128)} %get-tuple-element.1087), custom_call_target="InvertDiagBlocksLowerTriangular" | custom-call | tf_op jit(solution)/shard_map/jvp(vmap())/triangular_solve | solution.py:149
  413.7 161.7 %while.79 = (s32[]{:T(128)}, f32[2,128,128]{2,1,0:T(8,128)}, f32[2,128,256]{2,1,0:T(8,128)S(1)}, f32[16,2,128,128]{3,2,1,0:T(8,128)}, f32[16,2,128,256]{3,2,1,0:...) while((s32[]{:T(128)}, f32[2,128,128]{2,1,0:T(8,128)}, ...), condition=%wide.region_7.8_spmd.clone, body=%wide.region_6.7_spmd.clone.sunk | while | flops 226787328 | bytes 3477176 | solution.py:187
  578.1 30.7 %all_gather.87 = bf16[4,2,128]{0,1,2:T(2,128)(2,1)S(1)} all-gather(bf16[4,2,16]{0,1,2:T(2,128)(2,1)S(1)} %copy.402), channel_id=1, replica_groups=mesh['fsdp'=8,'tp'=4] {'fsdp'}, dimensions={2}, use_global_device_ids=true | all-gather | bytes 2304 | tf_op jit(solution)/shard_map/all_gather | solution.py:316
  710.9 33.9 %all-gather.26.cloned.1.call-done = bf16[512,1024]{1,0:T(8,128)(2,1)} async-done(((bf16[512,128]{1,0:T(8,128)(2,1)}), bf16[512,1024]{1,0:T(8,128)(2,1)}) %all-gather.26.cloned.1.call-update) | async-done | bytes 1048592 | tf_op jit(solution)/shard_map/all_gather | solution.py:320
  749.7 43.7 %reduce-scatter.36.cloned.1.call-done = f32[256,1024]{1,0:T(8,128)} async-done(((f32[1024,1024]{1,0:T(8,128)}), f32[256,1024]{1,0:T(8,128)}) %reduce-scatter.36.cloned.1.call-update) | async-done | bytes 1048592 | tf_op jit(solution)/shard_map/reduce_scatter | solution.py:418
  835.7 39.9 %all-gather.30.cloned.1.call-done = bf16[1024,704]{0,1:T(8,128)(2,1)} async-done(((bf16[128,704]{0,1:T(8,128)(2,1)}), bf16[1024,704]{0,1:T(8,128)(2,1)}) %all-gather.30.cloned.1.call-update) | async-done | bytes 1441808 | tf_op jit(solution)/shard_map/all_gather | solution.py:322
  880.9 37.8 %all-gather.32.cloned.1.call-done = bf16[1024,704]{0,1:T(8,128)(2,1)} async-done(((bf16[128,704]{0,1:T(8,128)(2,1)}), bf16[1024,704]{0,1:T(8,128)(2,1)}) %all-gather.32.cloned.1.call-update) | async-done | bytes 1441808 | tf_op jit(solution)/shard_map/all_gather | solution.py:323
  923.9 38.0 %all-gather.34.cloned.1.call-done = bf16[704,1024]{1,0:T(8,128)(2,1)} async-done(((bf16[704,128]{1,0:T(8,128)(2,1)}), bf16[704,1024]{1,0:T(8,128)(2,1)}) %all-gather.34.cloned.1.call-update) | async-done | bytes 1441808 | tf_op jit(solution)/shard_map/all_gather | solution.py:324
  1001.7 44.7 %reduce-scatter.40.cloned.1.call-done = f32[256,1024]{1,0:T(8,128)} async-done(((f32[1024,1024]{1,0:T(8,128)}), f32[256,1024]{1,0:T(8,128)}) %reduce-scatter.40.cloned.1.call-update) | async-done | bytes 1048592 | tf_op jit(solution)/shard_map/reduce_scatter | solution.py:443
  1127.1 34.0 %all-gather.2 = bf16[16,128,128]{2,1,0:T(8,128)(2,1)} all-gather(bf16[2,128,128]{2,1,0:T(8,128)(2,1)S(1)} %bitcast.568), channel_id=4, replica_groups=mesh['fsdp'=8,'tp'=4] {'fsdp'}, dimensions={0}, use_global_device_ids=true | all-gather | bytes 589824 | tf_op jit(solution)/shard_map/all_gather | solution.py:40
  1211.1 300.1 %while.78 = (s32[]{:T(128)}, f32[2,128,128]{2,1,0:T(8,128)}, f32[2,128,256]{2,1,0:T(8,128)S(1)}, f32[16,2,64]{2,0,1:T(8,128)}, f32[16,2,64,256]{3,2,0,1:T(8,128)...) while((s32[]{:T(128)}, f32[2,128,128]{2,1,0:T(8,128)}, ...), condition=%wide.region_21.22_spmd.clone, body=%wide.region_19.21_spmd.clone.sunk | while | flops 453296128 | bytes 5053173 | solution.py:187
  1681.0 63.6 %reduce-scatter.52.cloned.1.call-done = bf16[128,2]{1,0:T(8,128)(2,1)} async-done(((bf16[1024,2]{1,0:T(8,128)(2,1)}), bf16[128,2]{1,0:T(8,128)(2,1)}) %reduce-scatter.52.cloned.1.call-update) | async-done | bytes 528
  1746.0 63.7 %reduce-scatter.54.cloned.1.call-done = bf16[128,2]{1,0:T(8,128)(2,1)} async-done(((bf16[1024,2]{1,0:T(8,128)(2,1)}), bf16[128,2]{1,0:T(8,128)(2,1)}) %reduce-scatter.54.cloned.1.call-update) | async-done | bytes 528
  1811.0 63.9 %reduce-scatter.60.cloned.1.call-done = bf16[32,8]{1,0:T(8,128)(2,1)} async-done(((bf16[256,8]{1,0:T(8,128)(2,1)}), bf16[32,8]{1,0:T(8,128)(2,1)}) %reduce-scatter.60.cloned.1.call-update) | async-done | bytes 528
  1911.1 30.6 %reduce-scatter.62.cloned.1.call-done = bf16[128,512]{1,0:T(8,128)(2,1)} async-done(((bf16[1024,512]{1,0:T(8,128)(2,1)}), bf16[128,512]{1,0:T(8,128)(2,1)}) %reduce-scatter.62.cloned.1.call-update) | async-done | bytes 131088
  1943.4 64.6 %reduce-scatter.50.cloned.1.call-done = bf16[128,512]{1,0:T(8,128)(2,1)} async-done(((bf16[1024,512]{1,0:T(8,128)(2,1)}), bf16[128,512]{1,0:T(8,128)(2,1)}) %reduce-scatter.50.cloned.1.call-update) | async-done | bytes 131088 | tf_op jit(solution)/shard_map/reduce_scatter | solution.py:534
  2009.7 63.2 %reduce-scatter.44.cloned.1.call-done = bf16[128,256]{1,0:T(8,128)(2,1)} async-done(((bf16[1024,256]{1,0:T(8,128)(2,1)}), bf16[128,256]{1,0:T(8,128)(2,1)}) %reduce-scatter.44.cloned.1.call-update) | async-done | bytes 65552 | tf_op jit(solution)/shard_map/reduce_scatter | solution.py:525
  2074.4 63.5 %reduce-scatter.46.cloned.1.call-done = bf16[128,256]{1,0:T(8,128)(2,1)} async-done(((bf16[1024,256]{1,0:T(8,128)(2,1)}), bf16[128,256]{1,0:T(8,128)(2,1)}) %reduce-scatter.46.cloned.1.call-update) | async-done | bytes 65552 | tf_op jit(solution)/shard_map/reduce_scatter | solution.py:528
  2139.5 65.1 %reduce-scatter.48.cloned.1.call-done = bf16[128,512]{1,0:T(8,128)(2,1)} async-done(((bf16[1024,512]{1,0:T(8,128)(2,1)}), bf16[128,512]{1,0:T(8,128)(2,1)}) %reduce-scatter.48.cloned.1.call-update) | async-done | bytes 131088 | tf_op jit(solution)/shard_map/reduce_scatter | solution.py:531
  2206.2 30.9 %reduce-scatter.42.cloned.1.call-done = bf16[256,1024]{1,0:T(8,128)(2,1)} async-done(((bf16[1024,1024]{1,0:T(8,128)(2,1)}), bf16[256,1024]{1,0:T(8,128)(2,1)}) %reduce-scatter.42.cloned.1.call-update) | async-done | bytes 524304 | tf_op jit(solution)/shard_map/reduce_scatter | solution.py:496
  (1120 shorter events, 1152.9 us)
Async XLA Ops:
  7.2 198.1 %all-gather.20.cloned.1.call-start = ((), (), s32[]{:S(2)}) async-start(), calls=%async_computation.17 | async-start | bytes 2621440 | tf_op jit(solution)/shard_map/all_gather | solution.py:345
  7.9 203.8 %all-gather.22.cloned.1.call-start = ((), (), s32[]{:S(2)}) async-start(), calls=%async_computation.18 | async-start | bytes 1179648 | tf_op jit(solution)/shard_map/all_gather | solution.py:312
  8.7 638.6 %all-gather.40.cloned.1.call-start = ((), (), s32[]{:S(2)}) async-start(), calls=%async_computation.35 | async-start | bytes 1179648 | tf_op jit(solution)/shard_map/all_gather | solution.py:23
  576.1 129.6 %all-gather.24.cloned.1.call-start = ((), (), s32[]{:S(2)}) async-start(), calls=%async_computation.19 | async-start | bytes 1179648 | tf_op jit(solution)/shard_map/all_gather | solution.py:313
  576.7 168.1 %all-gather.26.cloned.1.call-start = ((), (), s32[]{:S(2)}) async-start(), calls=%async_computation.20 | async-start | bytes 1179648 | tf_op jit(solution)/shard_map/all_gather | solution.py:320
  577.2 216.2 %reduce-scatter.36.cloned.1.call-start = ((), (), s32[]{:S(2)}) async-start(), calls=%async_computation.21 | async-start | bytes 5242880 | tf_op jit(solution)/shard_map/reduce_scatter | solution.py:418
  797.3 164.7 %all-gather.34.cloned.1.call-start = ((), (), s32[]{:S(2)}) async-start(), calls=%async_computation.25 | async-start | bytes 1622016 | tf_op jit(solution)/shard_map/all_gather | solution.py:324
  798.0 186.1 %all-gather.36.cloned.1.call-start = ((), (), s32[]{:S(2)}) async-start(), calls=%async_computation.27 | async-start | bytes 2621440 | tf_op jit(solution)/shard_map/all_gather | solution.py:346
  798.6 247.9 %reduce-scatter.40.cloned.1.call-start = ((), (), s32[]{:S(2)}) async-start(), calls=%async_computation.28 | async-start | bytes 5242880 | tf_op jit(solution)/shard_map/reduce_scatter | solution.py:443
  1048.7 141.4 %all-gather.44.cloned.1.call-start = ((), (), s32[]{:S(2)}) async-start(), calls=%async_computation.37 | async-start | bytes 1179648 | tf_op jit(solution)/shard_map/all_gather | solution.py:40
  1102.8 536.7 %reduce-scatter.64.cloned.1.call-start = ((), (), s32[]{:S(2)}) async-start(), calls=%async_computation.44 | async-start | bytes 1769472
  1110.3 531.1 %reduce-scatter.66.cloned.1.call-start = ((), (), s32[]{:S(2)}) async-start(), calls=%async_computation.45 | async-start | bytes 1769472
  1117.8 525.4 %reduce-scatter.68.cloned.1.call-start = ((), (), s32[]{:S(2)}) async-start(), calls=%async_computation.46 | async-start | bytes 1769472
  1125.3 519.8 %reduce-scatter.38.cloned.1.call-start = ((), (), s32[]{:S(2)}) async-start(), calls=%async_computation.26 | async-start | bytes 2621440 | tf_op jit(solution)/shard_map/reduce_scatter | solution.py:429
  1166.1 481.8 %reduce-scatter.56.cloned.1.call-start = ((), (), s32[]{:S(2)}) async-start(), calls=%async_computation.40 | async-start | bytes 36864
  1573.0 171.5 %reduce-scatter.52.cloned.1.call-start = ((), (), s32[]{:S(2)}) async-start(), calls=%async_computation.38 | async-start | bytes 294912
  1575.6 234.1 %reduce-scatter.54.cloned.1.call-start = ((), (), s32[]{:S(2)}) async-start(), calls=%async_computation.39 | async-start | bytes 294912
  1576.9 298.1 %reduce-scatter.60.cloned.1.call-start = ((), (), s32[]{:S(2)}) async-start(), calls=%async_computation.42 | async-start | bytes 73728
  1578.1 363.6 %reduce-scatter.62.cloned.1.call-start = ((), (), s32[]{:S(2)}) async-start(), calls=%async_computation.43 | async-start | bytes 1179648
  1584.3 423.7 %reduce-scatter.50.cloned.1.call-start = ((), (), s32[]{:S(2)}) async-start(), calls=%async_computation.34 | async-start | bytes 1179648 | tf_op jit(solution)/shard_map/reduce_scatter | solution.py:534
  1586.8 486.2 %reduce-scatter.44.cloned.1.call-start = ((), (), s32[]{:S(2)}) async-start(), calls=%async_computation.31 | async-start | bytes 589824 | tf_op jit(solution)/shard_map/reduce_scatter | solution.py:525
  1605.5 532.4 %reduce-scatter.46.cloned.1.call-start = ((), (), s32[]{:S(2)}) async-start(), calls=%async_computation.32 | async-start | bytes 589824 | tf_op jit(solution)/shard_map/reduce_scatter | solution.py:528
  1614.9 589.6 %reduce-scatter.48.cloned.1.call-start = ((), (), s32[]{:S(2)}) async-start(), calls=%async_computation.33 | async-start | bytes 1179648 | tf_op jit(solution)/shard_map/reduce_scatter | solution.py:531
  1624.6 612.5 %reduce-scatter.42.cloned.1.call-start = ((), (), s32[]{:S(2)}) async-start(), calls=%async_computation.30 | async-start | bytes 2621440 | tf_op jit(solution)/shard_map/reduce_scatter | solution.py:496
  (186 other events, 3677.5 us)
Sparse Core Ops, SparseCore 0:
  37.0 43.3 all-gather.21
  575.5 37.5 all-gather.39
  615.7 48.1 all-gather.41
  665.9 38.7 all-gather.23
  706.6 38.0 all-gather.25
  749.8 43.5 reduce-scatter.35
  832.6 42.9 all-gather.29
  877.5 41.1 all-gather.31
  920.7 41.1 all-gather.33
  1001.8 44.5 reduce-scatter.39
  1103.0 42.2 all-gather.43
  1148.5 65.1 reduce-scatter.63
  1216.9 64.4 reduce-scatter.65
  1284.7 64.3 reduce-scatter.67
  1571.1 50.8 reduce-scatter.55
  1625.7 53.7 reduce-scatter.57
  1683.4 61.1 reduce-scatter.51
  1748.5 61.1 reduce-scatter.53
  1813.4 61.4 reduce-scatter.59
  1878.4 63.2 reduce-scatter.61
  1945.0 63.0 reduce-scatter.49
  2011.3 61.6 reduce-scatter.43
  2076.3 61.6 reduce-scatter.45
  2141.4 63.1 reduce-scatter.47
  (6 shorter events, 163.0 us)
where the time goes:
time: 2260 us; the launch traced here: 2250 us
  waiting for transfers between devices  860 us (38%)
  matrix products  519 us (23%)
  blocking collectives  316 us (14%)
  other arithmetic  271 us (12%)
  local copies, waits for them, and re-layouts  242 us (11%)
    unnamed x39, waiting for transfers between devices  257 us
    another operation x5, other arithmetic, block_terms(): lax.linalg.triangular_solve(lower_mat, beta_block[:, :, None] * value_blo...  162 us
    dot_general x30, matrix products, mat_dot(): return jnp.dot(left, right, preferred_element_type=jnp.float32)  99.6 us
    dot_general x48, matrix products, advance(): jnp.dot(last_block.T, key_block, precision=highest)  87.5 us
    dot_general x48, matrix products, advance(): jnp.dot(last_block.T, value_block, precision=highest)  81 us
    dot_general x48, matrix products, advance(): new_matrix = jnp.dot(transfer, matrix, precision=highest)  67.8 us
    reduce_scatter x1, waiting for transfers between devices, shards(): lax.psum_scatter(grad_value.astype(jnp.bfloat16), 'fsdp', scatter_dimensi...  65.1 us
    reduce_scatter x1, waiting for transfers between devices, shards(): lax.psum_scatter(grad_gate_out.astype(jnp.bfloat16), 'fsdp', scatter_dime...  64.6 us
  transfers between devices with their start and end apart: 32, of which 21 were waited for; matrix products, arithmetic and copies ran while one was open for 28% of the time, Pallas kernels for 0%

commit v1 on v0

v1 whole, which is shorter than its diff:
```python
import jax
import jax.numpy as jnp
from jax import lax
from jax.sharding import PartitionSpec as P

K = 128
V = 256
CONV = 4
GROUP = 128
MAXLEN = 4096


highest = lax.Precision.HIGHEST
high = lax.Precision.HIGH


def shifted(array, axis, by):
    count = lax.axis_size(axis)
    pairs = [(i, i + by) for i in range(count) if 0 <= i + by < count]
    return lax.ppermute(array, axis, pairs)


def mat_dot(left, right):
    return jnp.dot(left, right, preferred_element_type=jnp.float32)


def rms_scale(values, scale_gain):
    return (
        values * lax.rsqrt(jnp.mean(values * values, axis=-1, keepdims=True) + 1e-06) * scale_gain
    )


def unit_rows(values):
    return values * lax.rsqrt(jnp.sum(values * values, axis=-1, keepdims=True) + 1e-06)


def seq_begin(lengths, positions):
    offsets = jnp.cumsum(lengths) - lengths
    chosen = jnp.where(offsets[None, :] <= positions[:, None], offsets[None, :], 0)
    return jnp.max(chosen, axis=1)


def split_heads(flat, width):
    return flat.reshape(flat.shape[0], -1, width).transpose(1, 0, 2)


def merge_heads(stacked):
    return stacked.transpose(1, 0, 2).reshape(stacked.shape[1], -1)


def short_conv(inputs, rim_rows, kernel, begins, positions):
    row_count = inputs.shape[0]
    padded = jnp.concatenate([rim_rows, inputs], axis=0)
    result = kernel[0] * inputs
    for lag_step in range(1, CONV):
        in_range = (positions - lag_step >= begins).astype(inputs.dtype)[:, None]
        start_row = CONV - 1 - lag_step
        result = result + kernel[lag_step] * padded[start_row : start_row + row_count] * in_range
    return jax.nn.silu(result)


def head_inputs(
    query_raw,
    key_raw,
    value_raw,
    query_rim,
    key_rim,
    value_rim,
    query_kernel,
    key_kernel,
    value_kernel,
    beta_raw,
    decay_raw,
    decay_scale,
    decay_shift,
    begins,
    positions,
):
    query_vec = unit_rows(
        short_conv(query_raw, query_rim, query_kernel, begins, positions)
    ) * query_raw.shape[1] ** (-0.5)
    key_vec = unit_rows(short_conv(key_raw, key_rim, key_kernel, begins, positions))
    value_vec = short_conv(value_raw, value_rim, value_kernel, begins, positions)
    beta_gate = jax.nn.sigmoid(beta_raw)
    decay_rate = -jnp.exp(decay_scale) * jax.nn.softplus(decay_raw + decay_shift)
    return (query_vec, key_vec, value_vec, beta_gate, decay_rate)


def level_mask(size, step):
    row = lax.broadcasted_iota(jnp.int32, (size, size), 0) // step
    col = lax.broadcasted_iota(jnp.int32, (size, size), 1) // step
    return ((row // 2 == col // 2) & (row > col)).astype(jnp.float32)


@jax.custom_vjp
def unit_lower_inverse(strict_lower):
    size = strict_lower.shape[-1]
    inverse = jnp.eye(size, dtype=strict_lower.dtype) - strict_lower * level_mask(size, 1)
    step = 2
    while step < size:
        corner = strict_lower * level_mask(size, step)
        inverse = inverse - jnp.matmul(
            jnp.matmul(inverse, corner, precision=high), inverse, precision=high
        )
        step = step * 2
    return inverse


def unit_lower_inverse_fwd(strict_lower):
    inverse = unit_lower_inverse(strict_lower)
    return inverse, inverse


def unit_lower_inverse_bwd(inverse, grad):
    flipped = jnp.swapaxes(inverse, -1, -2)
    return (-jnp.matmul(jnp.matmul(flipped, grad, precision=high), flipped, precision=high),)


unit_lower_inverse.defvjp(unit_lower_inverse_fwd, unit_lower_inverse_bwd)


def block_terms(query_vec, key_vec, value_vec, beta_gate, decay_rate, begins, positions):
    blocks = query_vec.shape[0] // GROUP
    query_block = query_vec.reshape(blocks, GROUP, -1)
    key_block = key_vec.reshape(blocks, GROUP, -1)
    value_block = value_vec.reshape(blocks, GROUP, -1)
    beta_block = beta_gate.reshape(blocks, GROUP)
    decay_block = decay_rate.reshape(blocks, GROUP)
    begin_block = begins.reshape(blocks, GROUP)
    place_block = positions.reshape(blocks, GROUP)
    upper = jnp.triu(jnp.ones((GROUP, GROUP), decay_block.dtype))
    cumul = jnp.dot(decay_block, upper, precision=highest)
    same_seq = (begin_block[:, :, None] <= place_block[:, None, :]) & (
        place_block[:, None, :] <= place_block[:, :, None]
    )
    same_float = same_seq.astype(query_vec.dtype)
    factor = jnp.exp(jnp.where(same_seq, cumul[:, :, None] - cumul[:, None, :], 0.0)) * same_float
    alive_mask = (begin_block < place_block[:, :1]).astype(query_vec.dtype)
    carry_scale = jnp.exp(cumul) * alive_mask
    strict = (place_block[:, None, :] < place_block[:, :, None]).astype(query_vec.dtype)
    key_gram = jnp.einsum("ntd,nsd->nts", key_block, key_block, precision=high)
    inverse = unit_lower_inverse(beta_block[:, :, None] * key_gram * factor * strict)
    value_part = jnp.matmul(inverse, beta_block[:, :, None] * value_block)
    key_part = jnp.matmul(inverse, (beta_block * carry_scale)[:, :, None] * key_block)
    scores = jnp.einsum("ntd,nsd->nts", query_block, key_block) * factor
    key_last = key_block * factor[:, -1, :, None]
    return (query_block, carry_scale, scores, value_part, key_part, key_last)


def state_maps(block_parts):
    _, carry_scale, _, value_part, key_part, key_last = block_parts
    maps = jnp.einsum("hncj,hnck->hnjk", key_last, key_part)
    offsets = jnp.einsum("hncj,hncv->hnjv", key_last, value_part)
    return carry_scale[:, :, -1][:, :, None, None], maps, offsets


def state_run(scales, maps, offsets):
    heads, blocks = maps.shape[:2]
    matrix = jnp.broadcast_to(jnp.eye(K, dtype=jnp.float32), (heads, K, K))
    pair = jnp.concatenate([matrix, jnp.zeros_like(offsets[:, 0])], axis=-1)
    drive = jnp.concatenate([jnp.zeros_like(maps), offsets], axis=-1)
    starts = []
    for block in range(blocks):
        starts.append(pair)
        pair = (
            scales[:, block] * pair
            + drive[:, block]
            - jnp.einsum("hij,hjv->hiv", maps[:, block], pair, precision=high)
        )
    return jnp.stack(starts, axis=1), pair


def adjoint_run(scales, maps, local_grads, last):
    blocks = maps.shape[1]
    after = [None] * blocks
    grad = last
    for block in reversed(range(blocks)):
        after[block] = grad
        grad = (
            scales[:, block] * grad
            + local_grads[:, block]
            - jnp.einsum("hji,hjv->hiv", maps[:, block], grad, precision=high)
        )
    return jnp.stack(after, axis=1), grad


def entering(pairs, axis, row_count):
    count, mine = (lax.axis_size(axis), lax.axis_index(axis))
    hops = min(count - 1, -(-MAXLEN // row_count))
    state = jnp.zeros_like(pairs[0][..., K:])
    for hop in range(hops, 0, -1):
        piece = lax.dynamic_index_in_dim(pairs, jnp.maximum(mine - hop, 0), 0, False)
        new = (
            jnp.einsum("hij,hjv->hiv", piece[..., :K], state, precision=high) + piece[..., K:]
        )
        state = jnp.where(mine >= hop, new, state)
    return state


def carried_in(pairs, grads, axis, row_count):
    count, mine = (lax.axis_size(axis), lax.axis_index(axis))
    hops = min(count - 1, -(-MAXLEN // row_count))
    grad = jnp.zeros(grads.shape[1:], jnp.float32)
    for hop in range(hops, 0, -1):
        source = jnp.minimum(mine + hop, count - 1)
        piece = lax.dynamic_index_in_dim(pairs, source, 0, False)
        own = lax.dynamic_index_in_dim(grads, source, 0, False).astype(jnp.float32)
        new = jnp.einsum("hji,hjv->hiv", piece[..., :K], grad, precision=high) + own
        grad = jnp.where(mine + hop < count, new, grad)
    return grad


def step_states(block_parts, start_states):
    _, carry_scale, _, value_part, key_part, key_last = block_parts
    update = value_part - jnp.einsum("hncj,hnjv->hncv", key_part, start_states)
    return carry_scale[:, :, -1][:, :, None, None] * start_states + jnp.einsum(
        "hncj,hncv->hnjv", key_last, update
    )


def front_all(
    mixed_raw,
    rim_raw,
    query_kernel,
    key_kernel,
    value_kernel,
    beta_raw,
    decay_raw,
    decay_scale,
    decay_shift,
    begins,
    positions,
    head_count,
):
    query_width = head_count * K

    def front_one_head(
        query_raw,
        key_raw,
        value_raw,
        query_rim,
        key_rim,
        value_rim,
        query_taps,
        key_taps,
        value_taps,
        beta_head,
        decay_head,
        scale_head,
        shift_head,
    ):
        inputs = head_inputs(
            query_raw,
            key_raw,
            value_raw,
            query_rim,
            key_rim,
            value_rim,
            query_taps,
            key_taps,
            value_taps,
            beta_head,
            decay_head,
            scale_head,
            shift_head,
            begins,
            positions,
        )
        return block_terms(*inputs, begins, positions)

    return jax.vmap(front_one_head)(
        split_heads(mixed_raw[:, :query_width], K),
        split_heads(mixed_raw[:, query_width : 2 * query_width], K),
        split_heads(mixed_raw[:, 2 * query_width :], V),
        split_heads(rim_raw[:, :query_width], K),
        split_heads(rim_raw[:, query_width : 2 * query_width], K),
        split_heads(rim_raw[:, 2 * query_width :], V),
        jnp.transpose(query_kernel, (1, 0, 2)),
        jnp.transpose(key_kernel, (1, 0, 2)),
        jnp.transpose(value_kernel, (1, 0, 2)),
        beta_raw.T,
        decay_raw.T,
        decay_scale,
        decay_shift,
    )


def back_all(block_parts, start_states, gate_heads, out_scale):
    query_block, carry_scale, scores, value_part, key_part, _ = block_parts
    update = value_part - jnp.einsum("hncj,hnjv->hncv", key_part, start_states)
    outputs = carry_scale[..., None] * jnp.einsum("hncj,hnjv->hncv", query_block, start_states)
    outputs = outputs + jnp.einsum("hnts,hnsv->hntv", scores, update)
    outputs = outputs.reshape(outputs.shape[0], -1, outputs.shape[-1])
    return rms_scale(outputs, out_scale) * jax.nn.silu(gate_heads)


def shards(
    tokens,
    lengths,
    attn_gain,
    w_query,
    w_key,
    w_value,
    w_gate_out,
    w_beta,
    w_decay,
    conv_query,
    conv_key,
    conv_value,
    decay_log,
    decay_bias,
    out_gain,
    w_out,
    ffn_gain,
    w_ffn_gate,
    w_ffn_up,
    w_ffn_down,
    cotangent,
):
    count = lax.axis_size("fsdp")
    shard_rows = tokens.shape[0]
    query_cols, value_cols = w_query.shape[1], w_value.shape[1]
    hidden_cols = w_ffn_gate.shape[1]
    head_count = query_cols // K
    mixed_cols = 2 * query_cols + value_cols
    raw_cols = mixed_cols + value_cols

    own_float = tokens.astype(jnp.float32)
    small = jnp.concatenate(
        [
            part.reshape(-1)
            for part in (attn_gain, ffn_gain, out_gain, conv_query, conv_key, conv_value)
        ]
    )
    small = lax.all_gather(small, "fsdp")
    smalls, at = ([], 0)
    for part in (attn_gain, ffn_gain, out_gain, conv_query, conv_key, conv_value):
        piece = small[:, at : at + part.size].astype(jnp.float32)
        at = at + part.size
        if part.ndim == 3:
            piece = piece.reshape((count,) + part.shape).transpose(1, 2, 0, 3)
            smalls.append(piece.reshape(part.shape[0], part.shape[1], -1))
        else:
            smalls.append(piece.reshape(-1))
    gain_one, gain_two, norm_out, query_taps, key_taps, value_taps = smalls
    mixer_w = lax.all_gather(
        jnp.concatenate([w_query, w_key, w_value, w_gate_out, w_beta, w_decay], axis=1),
        "fsdp",
        axis=0,
        tiled=True,
    )
    out_t = lax.all_gather(w_out.T, "fsdp", axis=0, tiled=True)
    ffn_gate_w = lax.all_gather(w_ffn_gate, "fsdp", axis=0, tiled=True)
    ffn_up_w = lax.all_gather(w_ffn_up, "fsdp", axis=0, tiled=True)
    down_t = lax.all_gather(w_ffn_down.T, "fsdp", axis=0, tiled=True)
    normed_one_own, pull_one = jax.vjp(rms_scale, own_float, gain_one)
    normed_one = lax.all_gather(
        normed_one_own.astype(jnp.bfloat16), "tp", axis=0, tiled=True
    )
    cot_rows = lax.all_gather(cotangent, "tp", axis=0, tiled=True)
    row_count = normed_one.shape[0]
    positions = lax.axis_index("fsdp") * row_count + jnp.arange(row_count, dtype=jnp.int32)
    begins = seq_begin(lengths, positions)
    raw = mat_dot(normed_one, mixer_w)
    mixed_raw = raw[:, :mixed_cols].astype(jnp.bfloat16)
    gate_raw = raw[:, mixed_cols:raw_cols]
    beta_raw = raw[:, raw_cols : raw_cols + head_count]
    decay_raw = raw[:, raw_cols + head_count :]
    rim_recv = shifted(mixed_raw[row_count - (CONV - 1) :], "fsdp", 1)

    def front_local(*inputs):
        return front_all(*inputs, begins, positions, head_count)

    block_parts, pull_front = jax.vjp(
        front_local,
        mixed_raw.astype(jnp.float32),
        rim_recv.astype(jnp.float32),
        query_taps,
        key_taps,
        value_taps,
        beta_raw,
        decay_raw,
        decay_log,
        decay_bias,
    )
    scales, maps, offsets = state_maps(block_parts)
    prefixes, final_pair = state_run(scales, maps, offsets)
    pairs = lax.all_gather(final_pair, "fsdp")
    state_in = entering(pairs, "fsdp", row_count)
    start_states = (
        jnp.einsum("hnij,hjv->hniv", prefixes[..., :K], state_in, precision=high)
        + prefixes[..., K:]
    )
    mixer_out, pull_back = jax.vjp(
        back_all, block_parts, start_states, split_heads(gate_raw, V), norm_out
    )
    normed_mixer = merge_heads(mixer_out).astype(jnp.bfloat16)
    mixer_part = lax.dot_general(
        normed_mixer, out_t, (((1,), (1,)), ((), ())), preferred_element_type=jnp.float32
    )
    mixer_own = lax.psum_scatter(
        mixer_part.astype(jnp.bfloat16), "tp", scatter_dimension=0, tiled=True
    ).astype(jnp.float32)
    hidden_own = own_float + mixer_own
    normed_two_own, pull_two = jax.vjp(rms_scale, hidden_own, gain_two)
    normed_two = lax.all_gather(
        normed_two_own.astype(jnp.bfloat16), "tp", axis=0, tiled=True
    )
    gate_pre = mat_dot(normed_two, ffn_gate_w)
    up_pre = mat_dot(normed_two, ffn_up_w)
    gate_sigmoid = jax.nn.sigmoid(gate_pre)
    activated = (gate_pre * gate_sigmoid * up_pre).astype(jnp.bfloat16)
    d_active = mat_dot(cot_rows, down_t)
    d_gate = (d_active * up_pre * gate_sigmoid * (1.0 + gate_pre * (1.0 - gate_sigmoid))).astype(
        jnp.bfloat16
    )
    d_upper = (d_active * gate_pre * gate_sigmoid).astype(jnp.bfloat16)
    d_normed_two = mat_dot(d_gate, ffn_gate_w.T) + mat_dot(d_upper, ffn_up_w.T)
    d_normed_two_own = lax.psum_scatter(
        d_normed_two.astype(jnp.bfloat16), "tp", scatter_dimension=0, tiled=True
    ).astype(jnp.float32)
    d_hidden_norm, gain_two_part = pull_two(d_normed_two_own)
    d_hidden = cotangent.astype(jnp.float32) + d_hidden_norm
    d_hidden_rows = lax.all_gather(d_hidden.astype(jnp.bfloat16), "tp", axis=0, tiled=True)
    ffn_part = mat_dot(activated, down_t.T)
    ffn_own = lax.psum_scatter(
        ffn_part.astype(jnp.bfloat16), "tp", scatter_dimension=0, tiled=True
    ).astype(jnp.float32)
    output = hidden_own + ffn_own

    def summed(grad):
        return lax.psum_scatter(
            grad.astype(jnp.bfloat16), "fsdp", scatter_dimension=0, tiled=True
        ).astype(jnp.float32)

    grad_w_ffn_gate = summed(mat_dot(normed_two.T, d_gate))
    grad_w_ffn_up = summed(mat_dot(normed_two.T, d_upper))
    grad_w_ffn_down = summed(mat_dot(cot_rows.T, activated)).T
    d_mixer = mat_dot(d_hidden_rows, out_t)
    grad_w_out = summed(mat_dot(d_hidden_rows.T, normed_mixer)).T
    d_parts, d_starts, d_gate_heads, norm_out_part = pull_back(split_heads(d_mixer, V))
    _, d_state_in = adjoint_run(scales, maps, d_starts, jnp.zeros_like(state_in))
    d_state_out = carried_in(
        pairs, lax.all_gather(d_state_in.astype(jnp.bfloat16), "fsdp"), "fsdp", row_count
    )
    d_next, _ = adjoint_run(scales, maps, d_starts, d_state_out)
    _, pull_step = jax.vjp(lambda parts: step_states(parts, start_states), block_parts)
    d_parts = jax.tree.map(jnp.add, d_parts, pull_step(d_next)[0])
    (
        d_mixed,
        d_rim,
        d_query_taps,
        d_key_taps,
        d_value_taps,
        d_beta_raw,
        d_decay_raw,
        d_decay_log,
        d_decay_bias,
    ) = pull_front(d_parts)
    rim_grad = shifted(d_rim, "fsdp", -1)
    d_mixed = d_mixed.at[row_count - (CONV - 1) :].add(rim_grad)
    d_raw = jnp.concatenate(
        [
            part.astype(jnp.bfloat16)
            for part in (d_mixed, merge_heads(d_gate_heads), d_beta_raw, d_decay_raw)
        ],
        axis=1,
    )
    d_normed_one = mat_dot(d_raw, mixer_w.T)
    d_normed_one_own = lax.psum_scatter(
        d_normed_one.astype(jnp.bfloat16), "tp", scatter_dimension=0, tiled=True
    ).astype(jnp.float32)
    d_rows_norm, gain_one_part = pull_one(d_normed_one_own)
    d_tokens = d_hidden + d_rows_norm
    grad_mixer_w = summed(mat_dot(normed_one.T, d_raw))
    cuts = (
        query_cols,
        2 * query_cols,
        mixed_cols,
        raw_cols,
        raw_cols + head_count,
    )
    grads_w = jnp.split(grad_mixer_w, cuts, axis=1)
    gains = lax.psum(jnp.concatenate([gain_one_part, gain_two_part, norm_out_part]), "tp")
    width = gain_one.shape[0]

    def spread(taps):
        taps = taps.reshape(taps.shape[0], taps.shape[1], count, -1)
        return taps.transpose(2, 0, 1, 3).reshape(count, -1)

    decay_pair = jnp.concatenate([d_decay_log, d_decay_bias])
    small_parts = [
        gains[:width].reshape(count, -1),
        gains[width : 2 * width].reshape(count, -1),
        gains[2 * width :].reshape(count, -1),
        spread(d_query_taps),
        spread(d_key_taps),
        spread(d_value_taps),
        jnp.broadcast_to(decay_pair[None, :], (count, decay_pair.shape[0])),
    ]
    small_sum = lax.psum_scatter(
        jnp.concatenate(small_parts, axis=1), "fsdp", scatter_dimension=0, tiled=True
    )[0]
    small_cuts, at = ([], 0)
    for part in small_parts[:-1]:
        at = at + part.shape[1]
        small_cuts.append(at)
    small_out = jnp.split(small_sum, small_cuts)
    return (
        output,
        d_tokens,
        small_out[0],
        *grads_w,
        small_out[3].reshape(conv_query.shape),
        small_out[4].reshape(conv_key.shape),
        small_out[5].reshape(conv_value.shape),
        small_out[6][:head_count],
        small_out[6][head_count:],
        small_out[2],
        grad_w_out,
        small_out[1],
        grad_w_ffn_gate,
        grad_w_ffn_up,
        grad_w_ffn_down,
    )


def solution(mesh):
    placed = (
        P(("fsdp", "tp"), None),
        P(),
        P("fsdp"),
        P("fsdp", "tp"),
        P("fsdp", "tp"),
        P("fsdp", "tp"),
        P("fsdp", "tp"),
        P("fsdp", "tp"),
        P("fsdp", "tp"),
        P(None, "tp", "fsdp"),
        P(None, "tp", "fsdp"),
        P(None, "tp", "fsdp"),
        P("tp"),
        P("tp"),
        P("fsdp"),
        P("tp", "fsdp"),
        P("fsdp"),
        P("fsdp", "tp"),
        P("fsdp", "tp"),
        P("tp", "fsdp"),
        P(("fsdp", "tp"), None),
    )
    return jax.shard_map(
        shards,
        mesh=mesh,
        in_specs=placed,
        out_specs=(
            P(("fsdp", "tp"), None),
            P(("fsdp", "tp"), None),
            P("fsdp"),
            P("fsdp", "tp"),
            P("fsdp", "tp"),
            P("fsdp", "tp"),
            P("fsdp", "tp"),
            P("fsdp", "tp"),
            P("fsdp", "tp"),
            P(None, "tp", "fsdp"),
            P(None, "tp", "fsdp"),
            P(None, "tp", "fsdp"),
            P("tp"),
            P("tp"),
            P("fsdp"),
            P("tp", "fsdp"),
            P("fsdp"),
            P("fsdp", "tp"),
            P("fsdp", "tp"),
            P("tp", "fsdp"),
        ),
        check_vma=False,
    )
```

time: 2260 us -> 1090 us (0.48)
  matrix products: 519 us -> 148 us
  waiting for transfers between devices: 860 us -> 628 us
  blocking collectives: 316 us -> 86.3 us
  other arithmetic: 271 us -> 81.8 us
  local copies, waits for them, and re-layouts: 242 us -> 114 us
    dot_general x227 -> x75, matrix products: 402 us -> 78.5 us  [the longest x3 8.34 us: back_all(): outputs = outputs + jnp.einsum('hnts,hnsv->hntv', scores, update)]
    all_gather x10 -> x0, blocking collectives: 268 us -> none  [the longest x1 34 us: carried_in(): lax.all_gather(a.astype(kind), axis)]
    reduce_scatter x7 -> x4, waiting for transfers between devices: 376 us -> 155 us  [the longest x1 63.5 us: summed(): lax.psum_scatter(grad.astype(jnp.bfloat16), 'fsdp', scatter_dimension=0,...]
    another operation x12 -> x1, other arithmetic: 164 us -> 0.18 us  [the longest x5 162 us: block_terms(): lax.linalg.triangular_solve(lower_mat, beta_block[:, :, None] * value_blo...]
    unnamed x39 -> x24, waiting for transfers between devices: 257 us -> 130 us
    all_gather x12 -> x10, waiting for transfers between devices: 199 us -> 311 us  [the longest x1 65.8 us: shards(): lax.all_gather(jnp.concatenate([w_query, w_key, w_value, w_gate_out, w_be...]
    while x79 -> x0, local copies, waits for them, and re-layouts: 61.9 us -> none
    dynamic_update_slice x48 -> x0, local copies, waits for them, and re-layouts: 55 us -> none  [state_run(): lax.scan(advance, start_pair, (carry_scale, value_part, key_part, key_last))]
  transfers between devices with their start and end apart: 32 -> 22, of which waited for: 21 -> 18; matrix products, arithmetic and copies ran while one was open for 28% -> 20% of each run, Pallas kernels for 0% -> 0%
where the time goes in v1:
time: 1090 us; the launch traced here: 1080 us
  waiting for transfers between devices  628 us (58%)
  matrix products  148 us (14%)
  local copies, waits for them, and re-layouts  114 us (10%)
  blocking collectives  86.3 us (8%)
  other arithmetic  81.8 us (8%)
  between operations  18.5 us (2%)
    unnamed x24, waiting for transfers between devices  130 us
    unnamed x2, blocking collectives  76.2 us
    dot_general x14, matrix products, mat_dot(): return jnp.dot(left, right, preferred_element_type=jnp.float32)  69.7 us
    all_gather x1, waiting for transfers between devices, shards(): lax.all_gather(jnp.concatenate([w_query, w_key, w_value, w_gate_out, w_be...  65.8 us
    reduce_scatter x1, waiting for transfers between devices, summed(): lax.psum_scatter(grad.astype(jnp.bfloat16), 'fsdp', scatter_dimension=0,...  63.5 us
    all_gather x1, waiting for transfers between devices, shards(): pairs = lax.all_gather(final_pair, 'fsdp')  56.3 us
    unnamed x452, local copies, waits for them, and re-layouts  47.5 us
    all_gather x1, waiting for transfers between devices, shards(): ffn_up_w = lax.all_gather(w_ffn_up, 'fsdp', axis=0, tiled=True)  39.8 us
  transfers between devices with their start and end apart: 22, of which 18 were waited for; matrix products, arithmetic and copies ran while one was open for 20% of the time, Pallas kernels for 0%

profile of v1, /device:TPU:0, one launch (start us, length us, event | category | flops | bytes accessed | tf_op | source)
XLA Modules:
  0.0 1082.8 jit_solution(15567366967778890842)
XLA Ops:
  14.1 38.8 %all-reduce.31 = bf16[6400]{0:T(1024)(128)(2,1)S(1)} all-reduce(bf16[6400]{0:T(1024)(128)(2,1)S(1)} %dynamic-update-slice.3), channel_id=2, replica_groups=mesh['fsdp'=8,'tp'=4] {'fsdp'}, use_global_device_ids=true, to_apply=%add.31 | all-reduce | flops 6400 | bytes 25600
  67.7 10.4 all-gather.15.cloned.1.call-done
  78.1 65.8 %all-gather.17.cloned.1.call-done = bf16[1024,1540]{1,0:T(8,128)(2,1)} async-done(((bf16[128,1540]{1,0:T(8,128)(2,1)}), bf16[1024,1540]{1,0:T(8,128)(2,1)}) %all-gather.17.cloned.1.call-update) | async-done | bytes 3153936 | tf_op jit(solution)/shard_map/all_gather | solution.py:346
  205.9 56.3 %all-gather.33.cloned.1.call-done = f32[16,128,384]{2,1,0:T(8,128)} async-done(((f32[2,128,384]{2,1,0:T(8,128)}), f32[16,128,384]{2,1,0:T(8,128)}) %all-gather.33.cloned.1.call-update) | async-done | bytes 3145744 | tf_op jit(solution)/shard_map/all_gather | solution.py:388
  283.7 18.5 %all-gather.19.cloned.1.call-done = bf16[1024,512]{0,1:T(8,128)(2,1)} async-done(((bf16[128,512]{0,1:T(8,128)(2,1)}), bf16[1024,512]{0,1:T(8,128)(2,1)}) %all-gather.19.cloned.1.call-update) | async-done | bytes 1048592 | tf_op jit(solution)/shard_map/all_gather | solution.py:352
  307.0 29.7 %reduce-scatter.18.cloned.1.call-done = bf16[256,1024]{1,0:T(8,128)(2,1)} async-done(((bf16[1024,1024]{1,0:T(8,128)(2,1)}), bf16[256,1024]{1,0:T(8,128)(2,1)}) %reduce-scatter.18.cloned.1.call-update) | async-done | bytes 524304 | tf_op jit(solution)/shard_map/reduce_scatter | solution.py:401
  343.9 37.8 %all-gather.23.cloned.1.call-done = bf16[1024,704]{0,1:T(8,128)(2,1)} async-done(((bf16[128,704]{0,1:T(8,128)(2,1)}), bf16[1024,704]{0,1:T(8,128)(2,1)}) %all-gather.23.cloned.1.call-update) | async-done | bytes 1441808 | tf_op jit(solution)/shard_map/all_gather | solution.py:353
  381.6 22.3 %all-gather.21.cloned.1.call-done = bf16[1024,1024]{1,0:T(8,128)(2,1)} async-done(((bf16[256,1024]{1,0:T(8,128)(2,1)}), bf16[1024,1024]{1,0:T(8,128)(2,1)}) %all-gather.21.cloned.1.call-update) | async-done | bytes 2097168 | tf_op jit(solution)/shard_map/all_gather | solution.py:406
  409.3 39.8 %all-gather.25.cloned.1.call-done = bf16[1024,704]{0,1:T(8,128)(2,1)} async-done(((bf16[128,704]{0,1:T(8,128)(2,1)}), bf16[1024,704]{0,1:T(8,128)(2,1)}) %all-gather.25.cloned.1.call-update) | async-done | bytes 1441808 | tf_op jit(solution)/shard_map/all_gather | solution.py:354
  454.3 38.0 %all-gather.27.cloned.1.call-done = bf16[1024,704]{0,1:T(8,128)(2,1)} async-done(((bf16[128,704]{0,1:T(8,128)(2,1)}), bf16[1024,704]{0,1:T(8,128)(2,1)}) %all-gather.27.cloned.1.call-update) | async-done | bytes 1441808 | tf_op jit(solution)/shard_map/all_gather | solution.py:355
  492.3 22.2 %all-gather.29.cloned.1.call-done = bf16[1024,1024]{1,0:T(8,128)(2,1)} async-done(((bf16[256,1024]{1,0:T(8,128)(2,1)}), bf16[1024,1024]{1,0:T(8,128)(2,1)}) %all-gather.29.cloned.1.call-update) | async-done | bytes 2097168 | tf_op jit(solution)/shard_map/all_gather | solution.py:360
  514.5 7.6 multiply_convert_fusion
  527.8 31.3 %reduce-scatter.22.cloned.1.call-done = bf16[256,1024]{1,0:T(8,128)(2,1)} async-done(((bf16[1024,1024]{1,0:T(8,128)(2,1)}), bf16[256,1024]{1,0:T(8,128)(2,1)}) %reduce-scatter.22.cloned.1.call-update) | async-done | bytes 524304 | tf_op jit(solution)/shard_map/reduce_scatter | solution.py:419
  569.6 18.7 %all-gather.31.cloned.1.call-done = bf16[1024,1024]{1,0:T(8,128)(2,1)} async-done(((bf16[256,1024]{1,0:T(8,128)(2,1)}), bf16[1024,1024]{1,0:T(8,128)(2,1)}) %all-gather.31.cloned.1.call-update) | async-done | bytes 2097168 | tf_op jit(solution)/shard_map/all_gather | solution.py:424
  696.8 6.9 multiply_reduce_fusion.17
  728.5 12.2 %collective-permute-done.1 = f32[3,1024]{0,1:T(8,128)S(1)} collective-permute-done((f32[3,1024]{0,1:T(8,128)S(1)}, f32[3,1024]{0,1:T(8,128)S(1)}, u32[]{:S(2)}, u32[]{:S(2)}) %collective-permute-start.1) | collective-permute-done | bytes 12320 | tf_op jit(solution)/shard_map/ppermute | solution.py:20
  747.1 8.8 concatenate.42
  755.9 8.4 convolution_convert_fusion.1
  790.7 65.8 %reduce-scatter.34.cloned.1.call-done = bf16[128,704]{1,0:T(8,128)(2,1)} async-done(((bf16[1024,704]{1,0:T(8,128)(2,1)}), bf16[128,704]{1,0:T(8,128)(2,1)}) %reduce-scatter.34.cloned.1.call-update) | async-done | bytes 180240
  859.2 63.5 %reduce-scatter.26.cloned.1.call-done = bf16[128,512]{1,0:T(8,128)(2,1)} async-done(((bf16[1024,512]{1,0:T(8,128)(2,1)}), bf16[128,512]{1,0:T(8,128)(2,1)}) %reduce-scatter.26.cloned.1.call-update) | async-done | bytes 131088 | tf_op jit(solution)/shard_map/reduce_scatter | solution.py:432
  924.5 30.8 %reduce-scatter.24.cloned.1.call-done = bf16[256,1024]{1,0:T(8,128)(2,1)} async-done(((bf16[1024,1024]{1,0:T(8,128)(2,1)}), bf16[256,1024]{1,0:T(8,128)(2,1)}) %reduce-scatter.24.cloned.1.call-update) | async-done | bytes 524304 | tf_op jit(solution)/shard_map/reduce_scatter | solution.py:470
  956.9 10.1 psum.7
  967.1 37.4 %all-reduce.32 = f32[8,804]{1,0:T(8,128)S(1)} all-reduce(f32[8,804]{1,0:T(8,128)S(1)} %concatenate.45), channel_id=9, replica_groups=mesh['fsdp'=8,'tp'=4] {'fsdp'}, use_global_device_ids=true, to_apply=%region_42.43.clone | all-reduce | flops 6432 | bytes 51456
  1014.5 55.9 %reduce-scatter.28.cloned.1.call-done = bf16[128,1540]{1,0:T(8,128)(2,1)} async-done(((bf16[1024,1540]{1,0:T(8,128)(2,1)}), bf16[128,1540]{1,0:T(8,128)(2,1)}) %reduce-scatter.28.cloned.1.call-update) | async-done | bytes 394256
  (751 shorter events, 327.4 us)
Async XLA Ops:
  7.3 70.9 %all-gather.15.cloned.1.call-start = ((), (), s32[]{:S(2)}) async-start(), calls=%async_computation.9 | async-start | bytes 2621440 | tf_op jit(solution)/shard_map/all_gather | solution.py:357
  58.1 85.8 %all-gather.17.cloned.1.call-start = ((), (), s32[]{:S(2)}) async-start(), calls=%async_computation.10 | async-start | bytes 3833856 | tf_op jit(solution)/shard_map/all_gather | solution.py:346
  59.4 202.8 %all-gather.33.cloned.1.call-start = ((), (), s32[]{:S(2)}) async-start(), calls=%async_computation.23 | async-start | bytes 3538944 | tf_op jit(solution)/shard_map/all_gather | solution.py:388
  152.4 6.7 collective-permute-start
  199.4 102.7 %all-gather.19.cloned.1.call-start = ((), (), s32[]{:S(2)}) async-start(), calls=%async_computation.11 | async-start | bytes 1179648 | tf_op jit(solution)/shard_map/all_gather | solution.py:352
  200.0 136.7 %reduce-scatter.18.cloned.1.call-start = ((), (), s32[]{:S(2)}) async-start(), calls=%async_computation.12 | async-start | bytes 2621440 | tf_op jit(solution)/shard_map/reduce_scatter | solution.py:401
  306.4 75.2 %all-gather.23.cloned.1.call-start = ((), (), s32[]{:S(2)}) async-start(), calls=%async_computation.14 | async-start | bytes 1622016 | tf_op jit(solution)/shard_map/all_gather | solution.py:353
  307.0 97.0 %all-gather.21.cloned.1.call-start = ((), (), s32[]{:S(2)}) async-start(), calls=%async_computation.13 | async-start | bytes 2621440 | tf_op jit(solution)/shard_map/all_gather | solution.py:406
  341.6 107.5 %all-gather.25.cloned.1.call-start = ((), (), s32[]{:S(2)}) async-start(), calls=%async_computation.15 | async-start | bytes 1622016 | tf_op jit(solution)/shard_map/all_gather | solution.py:354
  342.3 150.0 %all-gather.27.cloned.1.call-start = ((), (), s32[]{:S(2)}) async-start(), calls=%async_computation.16 | async-start | bytes 1622016 | tf_op jit(solution)/shard_map/all_gather | solution.py:355
  343.1 171.4 %all-gather.29.cloned.1.call-start = ((), (), s32[]{:S(2)}) async-start(), calls=%async_computation.18 | async-start | bytes 2621440 | tf_op jit(solution)/shard_map/all_gather | solution.py:360
  343.6 215.5 %reduce-scatter.22.cloned.1.call-start = ((), (), s32[]{:S(2)}) async-start(), calls=%async_computation.19 | async-start | bytes 2621440 | tf_op jit(solution)/shard_map/reduce_scatter | solution.py:419
  527.8 60.5 %all-gather.31.cloned.1.call-start = ((), (), s32[]{:S(2)}) async-start(), calls=%async_computation.20 | async-start | bytes 2621440 | tf_op jit(solution)/shard_map/all_gather | solution.py:424
  565.6 91.9 %all-gather.35.cloned.1.call-start = ((), (), s32[]{:S(2)}) async-start(), calls=%async_computation.24 | async-start | bytes 1179648 | tf_op jit(solution)/shard_map/all_gather | solution.py:444
  611.3 170.3 %reduce-scatter.30.cloned.1.call-start = ((), (), s32[]{:S(2)}) async-start(), calls=%async_computation.26 | async-start | bytes 1769472
  618.8 170.0 %reduce-scatter.32.cloned.1.call-start = ((), (), s32[]{:S(2)}) async-start(), calls=%async_computation.27 | async-start | bytes 1769472
  626.4 230.2 %reduce-scatter.34.cloned.1.call-start = ((), (), s32[]{:S(2)}) async-start(), calls=%async_computation.28 | async-start | bytes 1769472
  633.8 288.9 %reduce-scatter.26.cloned.1.call-start = ((), (), s32[]{:S(2)}) async-start(), calls=%async_computation.22 | async-start | bytes 1179648 | tf_op jit(solution)/shard_map/reduce_scatter | solution.py:432
  657.4 297.9 %reduce-scatter.24.cloned.1.call-start = ((), (), s32[]{:S(2)}) async-start(), calls=%async_computation.21 | async-start | bytes 2621440 | tf_op jit(solution)/shard_map/reduce_scatter | solution.py:470
  722.4 18.2 %collective-permute-start.1 = (f32[3,1024]{0,1:T(8,128)S(1)}, f32[3,1024]{0,1:T(8,128)S(1)}, u32[]{:S(2)}, u32[]{:S(2)}) collective-permute-start(f32[3,1024]{0,1:T(8,128)S(1)} %pad_add_fusion.4), channel_id=1, source_target_pairs={{4,0},{8,4},{12,8},{16,12},{20,16},{24,20},{28,24},{5,1},{9,5},{13... | collective-permute-start | bytes 36872 | tf_op jit(solution)/shard_map/ppermute | solution.py:20
  764.3 246.9 %reduce-scatter.20.cloned.1.call-start = ((), (), s32[]{:S(2)}) async-start(), calls=%async_computation.17 | async-start | bytes 2621440 | tf_op jit(solution)/shard_map/reduce_scatter | solution.py:426
  769.5 300.9 %reduce-scatter.28.cloned.1.call-start = ((), (), s32[]{:S(2)}) async-start(), calls=%async_computation.25 | async-start | bytes 3833856
  789.9 221.2 %copy-start.33 = (bf16[256,1024]{1,0:T(8,128)(2,1)S(1)}, bf16[256,1024]{1,0:T(8,128)(2,1)}, u32[]{:S(2)}) copy-start(bf16[256,1024]{1,0:T(8,128)(2,1)} %reduce-scatter.18.cloned.1.call-done) | copy-start | bytes 1572868
  789.9 221.2 %copy-start.52 = (bf16[256,1024]{1,0:T(8,128)(2,1)S(1)}, bf16[256,1024]{1,0:T(8,128)(2,1)}, u32[]{:S(2)}) copy-start(bf16[256,1024]{1,0:T(8,128)(2,1)} %param.43) | copy-start | bytes 1572868
  (211 other events, 5127.7 us)
Sparse Core Ops, SparseCore 0:
  58.2 19.8 all-gather.14
  80.9 62.9 all-gather.16
  199.6 62.5 all-gather.32
  264.0 38.0 all-gather.18
  306.5 30.1 reduce-scatter.17
  338.6 42.9 all-gather.22
  383.2 20.7 all-gather.20
  406.0 42.9 all-gather.24
  451.1 41.1 all-gather.26
  493.7 20.7 all-gather.28
  527.9 31.1 reduce-scatter.21
  565.7 22.5 all-gather.30
  611.4 40.2 all-gather.34
  655.0 64.3 reduce-scatter.29
  722.7 66.1 reduce-scatter.31
  792.1 64.4 reduce-scatter.33
  859.8 62.9 reduce-scatter.25
  925.1 30.1 reduce-scatter.23
  957.8 31.1 reduce-scatter.19
  992.5 77.9 reduce-scatter.27
